TPU v7x, 512 devices: a whole 4x8x8 slice. The times are simulated.
512 devices in a mesh: rep: 16 (over y_hi, x, core), shard: 32 (over y_lo, z).
Axes of the slice: x: 4, y: 8 (y_hi: 2, y_lo: 4; y = y_hi * 4 + y_lo), z: 8, core: 2. Of those that a mesh axis runs over, the one named last changes fastest.
Arguments:
- grad_blocks: float32 [16, 1664, 2048], P('rep', None, 'shard'), may hold values from -2400 to 2400
- gain_grads: float32 [16, 12800], P('rep', 'shard'), may hold values from -240 to 240
- first_moment: float32 [32, 106896], P('shard'), may hold values from -6 to 6
- second_moment: float32 [32, 106896], P('shard'), may hold values from 0.25 to 4
- master_flat: float32 [32, 106896], P('shard'), may hold values from -6 to 6
- ema_flat: float32 [32, 106896], P('shard'), may hold values from -6 to 6
Outputs:
- new_first: float32 [32, 106896], P('shard')
- new_second: float32 [32, 106896], P('shard')
- new_master: float32 [32, 106896], P('shard')
- new_ema: float32 [32, 106896], P('shard')
- weight_blocks: bfloat16 [2, 1664, 2048], P(None, None, 'shard')
- gains: bfloat16 [12800], replicated
All inputs are finite; a program needn't handle non-finite values.
Results may differ from a plain program's by a relative error of at most 0.0004.
Values may be sent and summed in bfloat16 or wider, within the bound.
A program may use at most 64 MiB of HBM per device.

v0:
```python
import jax
import jax.numpy as jnp
from jax import lax
from jax.sharding import PartitionSpec as P

STEP = 100
PARAMS = 3420672
beta_one = 0.9
beta_two = 0.95
adam_eps = 1e-08
learn_rate = 0.02
weight_decay = 0.1
ema_keep = 0.95
clip_eps = 1e-06


def shards(grad_blocks, gain_grads, first_moment, second_moment, master_flat, ema_flat):
    replicas = lax.axis_size("rep")
    matrix_part = grad_blocks[0]
    small_part = gain_grads[0]
    matrix_part, small_part = lax.psum((matrix_part, small_part), "rep")
    owned = lax.all_to_all(matrix_part, "shard", split_axis=0, concat_axis=1, tiled=True)
    partial_value = jnp.sum(owned * owned) + jnp.sum(small_part * small_part)
    total = lax.psum(partial_value, "shard") / (replicas * replicas)
    main_len = owned.shape[0] * owned.shape[1]
    grads = jnp.concatenate([owned.reshape(main_len), small_part]).reshape(1, -1) / replicas
    rms = jnp.sqrt(total / PARAMS)
    clip = jnp.minimum(1.0, 1.0 / (rms + clip_eps))
    clipped = grads * clip
    new_first = beta_one * first_moment + (1.0 - beta_one) * clipped
    new_second = beta_two * second_moment + (1.0 - beta_two) * clipped * clipped
    update = (
        new_first
        / (1.0 - beta_one**STEP)
        / (jnp.sqrt(new_second / (1.0 - beta_two**STEP)) + adam_eps)
    )
    column = jnp.arange(grads.shape[1], dtype=jnp.int32)[None, :]
    decayed = jnp.where(column < main_len, weight_decay * master_flat, 0.0)
    new_master = master_flat - learn_rate * (update + decayed)
    new_ema = ema_keep * ema_flat + (1.0 - ema_keep) * new_master
    weights = new_master[0, :main_len].reshape(owned.shape).astype(jnp.bfloat16)
    averaged = new_ema[0, :main_len].reshape(owned.shape).astype(jnp.bfloat16)
    stacked = jnp.stack([weights, averaged], axis=0)
    weight_blocks = lax.all_to_all(stacked, "shard", split_axis=2, concat_axis=1, tiled=True)
    gains = lax.all_gather(
        new_master[0, main_len:].astype(jnp.bfloat16), "shard", axis=0, tiled=True
    )
    return (new_first, new_second, new_master, new_ema, weight_blocks, gains)


def solution(mesh):
    return jax.shard_map(
        shards,
        mesh=mesh,
        in_specs=(
            P("rep", None, "shard"),
            P("rep", "shard"),
            P("shard", None),
            P("shard", None),
            P("shard", None),
            P("shard", None),
        ),
        out_specs=(
            P("shard", None),
            P("shard", None),
            P("shard", None),
            P("shard", None),
            P(None, None, "shard"),
            P(),
        ),
        check_vma=False,
    )
```

profile of v0, /device:TPU:32, one launch (start us, length us, event | category | flops | bytes accessed | tf_op | source)
XLA Modules:
  0.0 537.8 jit_solution(15047340786175874549)
XLA Ops:
  7.2 0.0 all-reduce.3.cloned.1.call-start
  7.2 3.5 all_to_all.25
  10.8 0.0 all-reduce.3.cloned.1.call-update
  10.8 188.7 %all-reduce.3.cloned.1.call-done = f32[32,52,64]{1,0,2:T(8,128)} async-done(((f32[32,52,64]{1,0,2:T(8,128)}), f32[32,52,64]{1,0,2:T(8,128)}) %all-reduce.3.cloned.1.call-update) | async-done | bytes 426000 | tf_op jit(solution)/shard_map/psum | solution.py:21
  199.4 1.8 copy.33
  201.3 1.3 reshape.115
  202.6 8.0 %all-to-all-start = ((f32[32,1,3328]{2,1,0:T(1,128)}), f32[32,1,3328]{2,1,0:T(1,128)S(1)}, u32[]{:S(2)}, u32[]{:S(2)}) async-start(f32[32,1,3328]{2,1,0:T(1,128)} %reshape.115), calls=%async_computation | async-start | bytes 851968 | tf_op jit(solution)/shard_map/all_to_all | solution.py:22
  210.6 0.0 copy-done.7
  210.6 48.1 %psum.22 = f32[400]{0:T(512)S(1)} all-reduce(f32[400]{0:T(512)S(1)} %bitcast.23), channel_id=1, replica_groups=mesh['rep'=16,'shard'=32] {'rep'}, use_global_device_ids=true, to_apply=%region_1.0 | all-reduce | flops 400 | bytes 3200 | tf_op jit(solution)/shard_map/psum | solution.py:21
  258.7 0.6 multiply_reduce_fusion.1
  259.3 0.0 all-to-all-done
  259.3 0.5 broadcast.66
  259.8 1.6 reduce.7
  261.4 0.3 reshape.116
  261.7 0.8 multiply_reduce_fusion
  263.8 80.5 %psum.23 = f32[]{:T(128)} all-reduce(f32[]{:T(128)S(6)} %add.30), channel_id=1, replica_groups=mesh['rep'=16,'shard'=32] {'shard'}, use_global_device_ids=true, to_apply=%region_4.0 | all-reduce | flops 1 | bytes 8 | tf_op jit(solution)/shard_map/psum | solution.py:24
  345.1 0.0 copy-start.6
  345.1 0.2 copy.34
  345.3 0.0 copy-start.4
  345.3 0.0 copy-start.5
  345.3 0.5 concatenate.18
  345.8 0.3 copy-done.6
  346.1 0.2 copy-done.4
  346.3 0.1 copy-done.5
  346.4 5.0 fusion.3
  351.4 0.7 copy-done.1
  352.2 1.2 slice_reduce_fusion
  353.4 0.1 convert_element_type.26
  353.5 0.0 copy-done.3
  353.5 0.7 multiply_add_fusion
  354.3 0.0 copy-done
  354.3 0.0 copy-start.2
  354.3 0.7 copy-done.2
  355.1 1.1 fusion.2
  356.2 0.1 convert_element_type.27
  356.3 0.8 copy.36
  357.1 0.8 copy.35
  358.0 2.8 fusion.5
  360.8 3.5 reshape.117
  364.3 3.9 all-to-all-start.1
  368.2 1.3 dynamic-slice
  370.2 0.7 slice_reduce_fusion.1
  370.9 0.3 dynamic-update-slice
  371.1 153.1 %all-reduce = bf16[12800]{0:T(1024)(128)(2,1)} all-reduce(bf16[12800]{0:T(1024)(128)(2,1)S(1)} %dynamic-update-slice), channel_id=2, replica_groups=mesh['rep'=16,'shard'=32] {'shard'}, use_global_device_ids=true, to_apply=%add | all-reduce | flops 12800 | bytes 51200 | tf_op jit(solution)/shard_map/all_gather | solution.py:45
  524.2 0.0 all-to-all-done.1
  524.2 3.3 reshape.118
  527.6 0.7 copy.42
  528.3 2.7 all_to_all.31
  (5 shorter events, 0.0 us)
Async XLA Ops:
  7.2 192.3 %all-reduce.3.cloned.1.call-start = ((), (), s32[]{:S(2)}) async-start(), calls=%async_computation.2 | async-start | bytes 2097152 | tf_op jit(solution)/shard_map/psum | solution.py:21
  201.3 9.3 %copy-start.7 = (f32[1,400]{1,0:T(1,128)S(1)}, f32[1,400]{1,0:T(1,128)}, u32[]{:S(2)}) copy-start(f32[1,400]{1,0:T(1,128)} %param.7) | copy-start | bytes 4804
  202.6 56.7 %all-to-all-start = ((f32[32,1,3328]{2,1,0:T(1,128)}), f32[32,1,3328]{2,1,0:T(1,128)S(1)}, u32[]{:S(2)}, u32[]{:S(2)}) async-start(f32[32,1,3328]{2,1,0:T(1,128)} %reshape.115), calls=%async_computation | async-start | bytes 851968 | tf_op jit(solution)/shard_map/all_to_all | solution.py:22
  345.1 1.0 copy-start.6
  345.3 1.0 copy-start.4
  345.3 1.2 copy-start.5
  351.4 0.8 copy-start.1
  351.4 2.9 copy-start
  351.4 2.1 copy-start.3
  354.3 0.8 copy-start.2
  364.3 159.9 %all-to-all-start.1 = ((bf16[32,2,3328]{2,1,0:T(2,128)(2,1)}), bf16[32,2,3328]{2,1,0:T(2,128)(2,1)S(1)}, u32[]{:S(2)}, u32[]{:S(2)}) async-start(bf16[32,2,3328]{2,1,0:T(2,128)(2,1)} %reshape.117), calls=%async_computation.1 | async-start | bytes 851968 | tf_op jit(solution)/shard_map/all_to_all | solution.py:44
Sparse Core Ops, SparseCore 0:
  10.9 188.4 all-reduce.2
where the time goes:
time: 538 us
  blocking collectives  282 us (52%)
  waiting for transfers between devices  189 us (35%)
  local copies, waits for them, and re-layouts  26.9 us (5%)
  between operations  16.9 us (3%)
  starting transfers between devices  11.9 us (2%)
  other arithmetic  11.6 us (2%)
    psum x1, waiting for transfers between devices, shards(): matrix_part, small_part = lax.psum((matrix_part, small_part), 'rep')  189 us
    all_gather x1, blocking collectives, shards(): lax.all_gather(new_master[0, main_len:].astype(jnp.bfloat16), 'shard', ax...  153 us
    psum x1, blocking collectives, shards(): total = lax.psum(partial_value, 'shard') / (replicas * replicas)  80.5 us
    psum x1, blocking collectives, shards(): matrix_part, small_part = lax.psum((matrix_part, small_part), 'rep')  48.1 us
    unnamed x23, local copies, waits for them, and re-layouts  12.1 us
  transfers between devices with their start and end apart: 3, of which 1 were waited for; matrix products, arithmetic and copies ran while one was open for 1% of the time, Pallas kernels for 0%

commit v1 on v0

--- a/solution.py
+++ b/solution.py
@@ -12,6 +12,13 @@
 weight_decay = 0.1
 ema_keep = 0.95
 clip_eps = 1e-06
+
+
+def all_by_exchange(block, name, along):
+    peers = lax.axis_size(name)
+    blocks = jnp.stack([block for _ in range(peers)])
+    blocks = lax.all_to_all(blocks, name, split_axis=0, concat_axis=0)
+    return jnp.concatenate(blocks, axis=along)
 
 
 def shards(grad_blocks, gain_grads, first_moment, second_moment, master_flat, ema_flat):
@@ -42,9 +49,7 @@
     averaged = new_ema[0, :main_len].reshape(owned.shape).astype(jnp.bfloat16)
     stacked = jnp.stack([weights, averaged], axis=0)
     weight_blocks = lax.all_to_all(stacked, "shard", split_axis=2, concat_axis=1, tiled=True)
-    gains = lax.all_gather(
-        new_master[0, main_len:].astype(jnp.bfloat16), "shard", axis=0, tiled=True
-    )
+    gains = all_by_exchange(new_master[0, main_len:].astype(jnp.bfloat16), "shard", 0)
     return (new_first, new_second, new_master, new_ema, weight_blocks, gains)
 
 

time: 538 us -> 408 us (0.76)
  the two profiles are of different devices: /device:TPU:32 before, /device:TPU:64 now
where the time goes in v1:
time: 408 us; the launch traced here: 407 us
  waiting for transfers between devices  200 us (49%)
  blocking collectives  124 us (30%)
  starting transfers between devices  28.2 us (7%)
  local copies, waits for them, and re-layouts  26.1 us (6%)
  between operations  16.3 us (4%)
  other arithmetic  12.6 us (3%)
    psum x1, waiting for transfers between devices, shards(): matrix_part, small_part = lax.psum((matrix_part, small_part), 'rep')  189 us
    psum x1, blocking collectives, shards(): total = lax.psum(partial_value, 'shard') / (replicas * replicas)  76.4 us
    psum x1, blocking collectives, shards(): matrix_part, small_part = lax.psum((matrix_part, small_part), 'rep')  47.7 us
    all_to_all x1, waiting for transfers between devices, shards(): lax.all_to_all(stacked, 'shard', split_axis=2, concat_axis=1, tiled=True)  10.8 us
    unnamed x20, local copies, waits for them, and re-layouts  10.6 us
    all_to_all x1, starting transfers between devices, shards(): lax.all_to_all(stacked, 'shard', split_axis=2, concat_axis=1, tiled=True)  10.3 us
    all_to_all x1, starting transfers between devices, shards(): lax.all_to_all(matrix_part, 'shard', split_axis=0, concat_axis=1, tiled=T...  9.92 us
  transfers between devices with their start and end apart: 4, of which 2 were waited for; matrix products, arithmetic and copies ran while one was open for 3% of the time, Pallas kernels for 0%

profile of v1, /device:TPU:64, one launch (start us, length us, event | category | flops | bytes accessed | tf_op | source)
XLA Modules:
  0.0 407.1 jit_solution(3982760112405161947)
XLA Ops:
  7.2 0.0 all-reduce.2.cloned.1.call-start
  7.2 3.5 all_to_all.29
  10.8 0.0 all-reduce.2.cloned.1.call-update
  10.8 189.0 %all-reduce.2.cloned.1.call-done = f32[32,52,64]{1,0,2:T(8,128)} async-done(((f32[32,52,64]{1,0,2:T(8,128)}), f32[32,52,64]{1,0,2:T(8,128)}) %all-reduce.2.cloned.1.call-update) | async-done | bytes 426000 | tf_op jit(solution)/shard_map/psum | solution.py:28
  199.8 1.8 copy.33
  201.6 1.3 reshape.120
  202.9 9.9 %all-to-all-start = ((f32[32,1,3328]{2,1,0:T(1,128)}), f32[32,1,3328]{2,1,0:T(1,128)S(1)}, u32[]{:S(2)}, u32[]{:S(2)}) async-start(f32[32,1,3328]{2,1,0:T(1,128)} %reshape.120), calls=%async_computation | async-start | bytes 851968 | tf_op jit(solution)/shard_map/all_to_all | solution.py:29
  212.8 47.7 %psum.22 = f32[400]{0:T(512)S(1)} all-reduce(f32[400]{0:T(512)S(1)} %bitcast.22), channel_id=1, replica_groups=mesh['rep'=16,'shard'=32] {'rep'}, use_global_device_ids=true, to_apply=%region_1.0 | all-reduce | flops 400 | bytes 3200 | tf_op jit(solution)/shard_map/psum | solution.py:28
  260.5 0.6 multiply_reduce_fusion.1
  261.1 0.0 all-to-all-done
  261.1 0.5 broadcast.71
  261.7 1.6 reduce.8
  263.3 0.3 reshape.121
  263.6 0.8 multiply_reduce_fusion
  265.7 76.4 %psum.23 = f32[]{:T(128)} all-reduce(f32[]{:T(128)S(6)} %add.30), channel_id=1, replica_groups=mesh['rep'=16,'shard'=32] {'shard'}, use_global_device_ids=true, to_apply=%region_4.0 | all-reduce | flops 1 | bytes 8 | tf_op jit(solution)/shard_map/psum | solution.py:31
  342.8 0.0 copy-start.5
  342.8 0.2 copy.34
  343.0 0.0 copy-start.3
  343.0 0.0 copy-start.4
  343.0 0.5 concatenate.18
  343.6 0.3 copy-done.5
  343.8 0.2 copy-done.3
  344.1 0.1 copy-done.4
  344.2 5.0 %fusion.3 = (bf16[1,106896]{1,0:T(2,128)(2,1)S(1)}, f32[1,106896]{1,0:T(1,128)S(1)}, f32[1,106896]{1,0:T(1,128)}, f32[1,106896]{1,0:T(1,128)}) fusion(f32[1,106896]{1,0:T(1,128)S(1)} %copy-done.3, f32[]{:T(128)S(6)} %mul.88, f32[1,400]{1,0:T(1,128)S(1)} %bitcast.21, f32[1,106496]{1,0:T(1,128)S(1)} %concatenate.18, f32[1,106896]{1,0:T(1,128)S(1)} %copy-done.4, ...), kind=kLoop, calls=%fused_computation.16 | loop fusion | flops 2137920 | bytes 3206884 | tf_op jit(solution)/shard_map/convert.2
  349.2 1.2 slice_reduce_fusion
  350.4 0.1 convert_element_type.26
  350.6 0.5 broadcast.72
  351.1 0.8 reduce.9
  351.9 0.7 reshape.124
  352.6 8.0 %all-to-all-start.2 = ((bf16[32,2,200]{2,1,0:T(2,128)(2,1)}), bf16[32,2,200]{2,1,0:T(2,128)(2,1)S(1)}, u32[]{:S(2)}, u32[]{:S(2)}) async-start(bf16[32,2,200]{2,1,0:T(2,128)(2,1)} %reshape.124), calls=%async_computation.2 | async-start | bytes 65536 | tf_op jit(solution)/shard_map/all_to_all | solution.py:20
  360.7 0.7 multiply_add_fusion
  361.4 0.0 copy-start.1
  361.4 0.7 copy-done.1
  362.2 1.1 fusion.2
  363.3 0.1 convert_element_type.27
  363.4 0.8 copy.36
  364.3 0.8 copy.35
  365.1 2.8 fusion.5
  367.9 3.5 reshape.122
  371.5 0.0 all-to-all-done.2
  371.5 10.3 %all-to-all-start.1 = ((bf16[32,2,3328]{2,1,0:T(2,128)(2,1)}), bf16[32,2,3328]{2,1,0:T(2,128)(2,1)S(1)}, u32[]{:S(2)}, u32[]{:S(2)}) async-start(bf16[32,2,3328]{2,1,0:T(2,128)(2,1)} %reshape.122), calls=%async_computation.1 | async-start | bytes 851968 | tf_op jit(solution)/shard_map/all_to_all | solution.py:51
  381.7 0.1 reshape.125
  381.8 0.2 reduce.4
  382.0 0.7 reshape.114
  382.8 10.8 %all-to-all-done.1 = bf16[32,2,3328]{2,1,0:T(2,128)(2,1)S(1)} async-done(((bf16[32,2,3328]{2,1,0:T(2,128)(2,1)}), bf16[32,2,3328]{2,1,0:T(2,128)(2,1)S(1)}, u32[]{:S(2)}, u32[]{:S(2)}) %all-to-all-start.1) | async-done | bytes 426016 | tf_op jit(solution)/shard_map/all_to_all | solution.py:51
  393.6 3.3 reshape.123
  396.9 0.7 copy.42
  397.6 2.7 all_to_all.35
  (8 shorter events, 0.1 us)
Async XLA Ops:
  7.2 192.6 %all-reduce.2.cloned.1.call-start = ((), (), s32[]{:S(2)}) async-start(), calls=%async_computation.3 | async-start | bytes 2097152 | tf_op jit(solution)/shard_map/psum | solution.py:28
  201.6 11.2 %copy-start.6 = (f32[1,400]{1,0:T(1,128)S(1)}, f32[1,400]{1,0:T(1,128)}, u32[]{:S(2)}) copy-start(f32[1,400]{1,0:T(1,128)} %param.7) | copy-start | bytes 4804
  202.9 58.2 %all-to-all-start = ((f32[32,1,3328]{2,1,0:T(1,128)}), f32[32,1,3328]{2,1,0:T(1,128)S(1)}, u32[]{:S(2)}, u32[]{:S(2)}) async-start(f32[32,1,3328]{2,1,0:T(1,128)} %reshape.120), calls=%async_computation | async-start | bytes 851968 | tf_op jit(solution)/shard_map/all_to_all | solution.py:29
  342.8 1.0 copy-start.5
  343.0 1.0 copy-start.3
  343.0 1.2 copy-start.4
  349.2 12.2 %copy-start = (f32[1,106896]{1,0:T(1,128)}, f32[1,106896]{1,0:T(1,128)S(1)}, u32[]{:S(2)}) copy-start(f32[1,106896]{1,0:T(1,128)S(1)} %get-tuple-element.7) | copy-start | bytes 1282756
  349.2 11.5 %copy-start.2 = (f32[1,106896]{1,0:T(1,128)S(1)}, f32[1,106896]{1,0:T(1,128)}, u32[]{:S(2)}) copy-start(f32[1,106896]{1,0:T(1,128)} %param.11) | copy-start | bytes 1282756
  352.6 18.8 %all-to-all-start.2 = ((bf16[32,2,200]{2,1,0:T(2,128)(2,1)}), bf16[32,2,200]{2,1,0:T(2,128)(2,1)S(1)}, u32[]{:S(2)}, u32[]{:S(2)}) async-start(bf16[32,2,200]{2,1,0:T(2,128)(2,1)} %reshape.124), calls=%async_computation.2 | async-start | bytes 65536 | tf_op jit(solution)/shard_map/all_to_all | solution.py:20
  361.4 0.8 copy-start.1
  371.5 22.1 %all-to-all-start.1 = ((bf16[32,2,3328]{2,1,0:T(2,128)(2,1)}), bf16[32,2,3328]{2,1,0:T(2,128)(2,1)S(1)}, u32[]{:S(2)}, u32[]{:S(2)}) async-start(bf16[32,2,3328]{2,1,0:T(2,128)(2,1)} %reshape.122), calls=%async_computation.1 | async-start | bytes 851968 | tf_op jit(solution)/shard_map/all_to_all | solution.py:51
Sparse Core Ops, SparseCore 0:
  10.9 188.8 all-reduce.1
